TPU v7x, 256 devices: a whole 4x4x8 slice. The times are simulated.
256 devices in a mesh: dp: 4 (over x), cls: 64 (over z, y, core).
Axes of the slice: x: 4, y: 4, z: 8, core: 2. Of those that a mesh axis runs over, the one named last changes fastest.
Arguments:
- embeddings: float32 [2048, 512], P('dp'), may hold values from -60 to 60, as said below
- classifier: float32 [1048576, 512], P(('dp', 'cls')), may hold values from -60 to 60, as said below
- labels: int32 [2048], replicated, may hold values from 0 to 1048575
- row_scale: float32 [2048], replicated, may hold values from 16 to 512
Outputs:
- loss: float32 [2048], P(('dp', 'cls'))
Inputs may be any that keep to these rules, and one draw needn't show every extreme that they name: `embeddings`: rows of different scales. `classifier`: rows of different scales.
All inputs are finite; a program needn't handle non-finite values.
Results may differ from a plain program's by a relative error of at most 0.0003.
Values sent between devices are 32-bit elements; how exact they have to be, the bound alone decides.
No kernel may reach another device: no remote copies, remote signals or barrier semaphores. Data moves between devices by JAX's collectives and lax.ppermute only.
A program may use at most 128 MiB of HBM per device.

v0:
```python
import math
import jax
import jax.numpy as jnp
from jax import lax
from jax.sharding import Mesh
from jax.sharding import PartitionSpec as P

DP_CLS = ("dp", "cls_0", "cls_1", "cls_2")
MARGIN = 0.5
COS_MARGIN = math.cos(MARGIN)
SIN_MARGIN = math.sin(MARGIN)


def gathered_once(shard, axis):
    leaves = jax.tree.leaves(shard)
    sequence = sorted(range(len(leaves)), key=lambda k: -leaves[k].size)
    width = (1, *leaves[sequence[0]].shape)[-1]
    lines = [
        jnp.pad(leaves[k].reshape(-1), (0, -leaves[k].size % width)).reshape(-1, width)
        for k in sequence
    ]
    both, at, found = (lax.all_gather(jnp.concatenate(lines), axis), 0, {})
    for k, line in zip(sequence, lines):
        section = both[:, at : at + len(line)].reshape(len(both), -1)
        found[k] = section[:, : leaves[k].size].reshape(-1, *leaves[k].shape)
        at += len(line)
    numbers = iter(range(len(leaves)))
    return jax.tree.map(lambda _: found[next(numbers)], shard)


def merged_by_axis(shard, axes, combine):
    for axis in axes:
        pieces = gathered_once(shard, axis)
        shard = jax.tree.map(lambda part: part[0], pieces)
        for k in range(1, lax.axis_size(axis)):
            shard = combine(shard, jax.tree.map(lambda part: part[k], pieces))
    return shard


def unit_rows(values):
    return values * lax.rsqrt(jnp.sum(values * values, axis=-1, keepdims=True) + 1e-06)


def margin_logit(units, picked, scales):
    cosine = jnp.sum(units * picked, axis=-1)
    across = units - cosine[:, None] * picked
    sine = jnp.sqrt(jnp.sum(across * across, axis=-1))
    return scales * (cosine * COS_MARGIN - sine * SIN_MARGIN)


def block_stats(units, rows, class_ids, labels, scales, picked, owned):
    cosine = lax.dot_general(
        units,
        rows,
        (((1,), (1,)), ((), ())),
        precision=lax.Precision.HIGHEST,
        preferred_element_type=jnp.float32,
    )
    target = margin_logit(units, picked, scales)
    hit = labels[:, None] == class_ids[None, :]
    logits = jnp.where(hit, target[:, None], scales[:, None] * cosine)
    peak = jnp.max(logits, axis=1)
    total = jnp.sum(jnp.exp(logits - peak[:, None]), axis=1)
    return (peak, total, jnp.where(owned, target, jnp.zeros_like(target)))


def merge_rows(first, second):
    peak = jnp.maximum(first[0], second[0])
    total = first[1] * jnp.exp(first[0] - peak) + second[1] * jnp.exp(second[0] - peak)
    return (peak, total, first[2] + second[2])


def body(embeddings, classifier, labels, row_scale):
    rows_here = classifier.shape[0]
    units_mine = unit_rows(embeddings)
    normed = unit_rows(classifier)
    offset = lax.axis_index(DP_CLS) * rows_here
    class_ids = offset + jnp.arange(rows_here, dtype=jnp.int32)
    owned_all = (labels >= offset) & (labels < offset + rows_here)
    local_all = jnp.clip(labels - offset, 0, rows_here - 1)
    count = labels.shape[0]
    picked = jnp.take(normed, local_all, axis=0)
    stats = block_stats(
        lax.all_gather(units_mine, "dp", axis=0, tiled=True),
        normed,
        class_ids,
        labels,
        row_scale,
        picked,
        owned_all,
    )
    peak, total, target = tuple((fresh for fresh in stats))
    share = count // lax.axis_size(DP_CLS)
    first = lax.axis_index(DP_CLS) * share
    peak, total, target = merged_by_axis((peak, total, target), DP_CLS, merge_rows)
    whole = peak + jnp.log(total) - target
    return lax.dynamic_slice_in_dim(whole, first, share)


def solution(mesh):
    torus = Mesh(mesh.devices.reshape(mesh.shape["dp"], 8, 4, 2), ("dp", "cls_0", "cls_1", "cls_2"))
    return jax.shard_map(
        body,
        mesh=torus,
        in_specs=(P("dp", None), P(DP_CLS, None), P(), P()),
        out_specs=P(DP_CLS),
        check_vma=False,
    )
```

profile of v0, /device:TPU:1, one launch (start us, length us, event | category | flops | bytes accessed | tf_op | source)
XLA Modules:
  0.0 210.5 jit_solution(7871280436764989805)
XLA Ops:
  6.5 0.0 all-gather.10.cloned.1.call-start
  6.5 1.4 multiply_reduce_fusion.3
  7.9 2.3 %broadcast_multiply_fusion.1 = f32[512,512]{1,0:T(8,128)} fusion(f32[512,512]{1,0:T(8,128)} %param.4, f32[512]{0:T(512)S(1)} %add_rsqrt_fusion.1), kind=kLoop, calls=%fused_computation.9 | loop fusion | flops 262144 | bytes 2099200 | tf_op jit(solution)/shard_map/mul | solution.py:41
  10.3 0.0 all-gather.10.cloned.1.call-update
  10.3 0.0 copy-start.1
  10.3 0.9 fusion.43
  11.2 4.1 %multiply_reduce_fusion = f32[4096]{0:T(1024)S(1)} fusion(f32[4096,512]{1,0:T(8,128)} %param.5), kind=kLoop, calls=%fused_computation.4 | loop fusion | flops 4190208 | bytes 8404992 | tf_op jit(solution)/shard_map/reduce_sum | solution.py:41
  15.3 0.8 copy-done.1
  16.1 3.6 %broadcast_multiply_fusion = f32[4096,512]{1,0:T(8,128)} fusion(f32[4096,512]{1,0:T(8,128)S(1)} %copy-done.1, f32[4096]{0:T(1024)S(1)} %add_rsqrt_fusion), kind=kLoop, calls=%fused_computation.7 | loop fusion | flops 2097152 | bytes 16793600 | tf_op jit(solution)/shard_map/mul | solution.py:41
  19.6 0.0 copy-start.3
  19.6 12.9 %gather_fusion = f32[2048,512]{1,0:T(8,128)} fusion(f32[4096,512]{1,0:T(8,128)} %broadcast_multiply_fusion, s32[2048]{0:T(1024)S(1)} %fusion.43), kind=kCustom, calls=%fused_computation | custom fusion | bytes 8396800 | tf_op jit(solution)/shard_map/jit(_take)/gather | solution.py:82
  32.6 0.0 copy-done.3
  32.6 0.0 copy-start.4
  32.6 32.2 %all-gather.10.cloned.1.call-done = f32[2048,512]{1,0:T(8,128)} async-done(((f32[512,512]{1,0:T(8,128)}), f32[2048,512]{1,0:T(8,128)}) %all-gather.10.cloned.1.call-update) | async-done | bytes 4194320 | tf_op jit(solution)/shard_map/all_gather | solution.py:84
  64.8 4.1 %multiply_reduce_fusion.2 = f32[2048]{0:T(1024)S(1)} fusion(f32[2048,512]{1,0:T(8,128)} %all-gather.10.cloned.1.call-done, f32[2048,512]{1,0:T(8,128)} %gather_fusion, pred[2048]{0:T(1024)(128)(4,1)S(1)} %compare_and_fusion), kind=kLoop, calls=%fused_computation.6 | loop fusion | flops 3143680 | bytes 8398848 | tf_op jit(solution)/shard_map/reduce_sum | solution.py:45
  68.9 0.6 copy-done
  69.5 3.6 %multiply_reduce_fusion.1 = f32[2048]{0:T(1024)S(1)} fusion(f32[2048,512]{1,0:T(8,128)} %all-gather.10.cloned.1.call-done, f32[2048,512]{1,0:T(8,128)S(1)} %copy-done, f32[2048]{0:T(1024)S(1)} %multiply_reduce_fusion.2, pred[2048]{0:T(1024)(128)(4,1)S(1)} %compare_and_fusion), kind=kLoop, calls=%fused_computation.5 | loop fusion | flops 5240832 | bytes 8407040 | tf_op jit(solution)/shard_map/reduce_sum | solution.py:47
  73.1 0.0 copy-done.4
  73.1 0.0 slice-done
  73.1 0.1 copy-done.2
  73.2 1.4 slice-done.1
  74.7 59.6 %fusion = (f32[2048]{0:T(1024)S(1)}, f32[2048,4096]{1,0:T(8,128)}) fusion(f32[2048]{0:T(1024)S(1)} %copy-done.4, f32[2048]{0:T(1024)S(1)} %get-tuple-element.14, s32[4096]{0:T(1024)S(1)} %iota_add_fusion, s32[2048]{0:T(1024)S(1)} %copy-done.3, f32[2048,512]{1,0:T(8,128)S(1)} %copy-done.2, f32[4096,512]{1,0:T(8,128)S(1)} %bitcast.325), kind=kOutput, calls=%fused_computation.3 | convolution fusion | flops 51573161984 | bytes 46186496 | tf_op jit(solution)/shard_map/dot_general | solution.py:52
  134.3 15.2 %exponential_reduce_fusion = f32[2048]{0:T(1024)S(1)} fusion(f32[2048,4096]{1,0:T(8,128)} %get-tuple-element.21, f32[2048]{0:T(1024)S(1)} %get-tuple-element.20, f32[2048]{0:T(1024)S(1)} %copy-done.4, f32[2048]{0:T(1024)S(1)} %get-tuple-element.14, s32[4096]{0:T(1024)S(1)} %iota_add_fusion, s32[2048]{0:T(1024)S(1)} %copy-done.3), kind=kLoop, calls=%fused_computation.1 | loop fusion | flops 41940992 | bytes 33611776 | tf_op jit(solution)/shard_map/reduce_sum | solution.py:63
  149.5 9.1 %all-gather.4 = f32[4,3,2048]{2,1,0:T(4,128)S(1)} all-gather(f32[1,3,2048]{2,1,0:T(4,128)S(1)} %maximum_bitcast_fusion), channel_id=2, replica_groups=mesh['dp'=4,'cls_0'=8,'cls_1'=4,'cls_2'=2] {'dp'}, dimensions={0}, use_global_device_ids=true | all-gather | bytes 122880 | tf_op jit(solution)/shard_map/all_gather | solution.py:22
  158.6 0.1 fusion.35
  158.7 20.3 %all-gather.5 = f32[8,3,2048]{2,1,0:T(4,128)S(1)} all-gather(f32[1,3,2048]{2,1,0:T(4,128)S(1)} %maximum_bitcast_fusion.1), channel_id=3, replica_groups=mesh['dp'=4,'cls_0'=8,'cls_1'=4,'cls_2'=2] {'cls_0'}, dimensions={0}, use_global_device_ids=true | all-gather | bytes 221184 | tf_op jit(solution)/shard_map/all_gather | solution.py:22
  179.0 0.1 fusion.11
  179.1 0.2 fusion.13
  179.3 9.7 %all-gather.6 = f32[4,3,2048]{2,1,0:T(4,128)S(1)} all-gather(f32[1,3,2048]{2,1,0:T(4,128)S(1)} %maximum_bitcast_fusion.2), channel_id=4, replica_groups=mesh['dp'=4,'cls_0'=8,'cls_1'=4,'cls_2'=2] {'cls_1'}, dimensions={0}, use_global_device_ids=true | all-gather | bytes 122880 | tf_op jit(solution)/shard_map/all_gather | solution.py:22
  189.1 0.1 fusion.3
  189.2 13.8 %all-gather.7 = f32[2,3,2048]{2,1,0:T(4,128)S(1)} all-gather(f32[1,3,2048]{2,1,0:T(4,128)S(1)} %maximum_bitcast_fusion.3), channel_id=5, replica_groups=mesh['dp'=4,'cls_0'=8,'cls_1'=4,'cls_2'=2] {'cls_2'}, dimensions={0}, use_global_device_ids=true | all-gather | bytes 73728 | tf_op jit(solution)/shard_map/all_gather | solution.py:22
  203.1 0.6 dynamic-slice_subtract_fusion
  (19 shorter events, 0.3 us)
Async XLA Ops:
  6.5 58.3 %all-gather.10.cloned.1.call-start = ((), (), s32[]{:S(2)}) async-start(), calls=%async_computation | async-start | bytes 5242880 | tf_op jit(solution)/shard_map/all_gather | solution.py:84
  10.3 5.8 %copy-start.1 = (f32[4096,512]{1,0:T(8,128)S(1)}, f32[4096,512]{1,0:T(8,128)}, u32[]{:S(2)}) copy-start(f32[4096,512]{1,0:T(8,128)} %param.5) | copy-start | bytes 25165828
  19.6 13.0 %copy-start.3 = (s32[2048]{0:T(1024)S(1)}, s32[2048]{0:T(1024)}, u32[]{:S(2)}) copy-start(s32[2048]{0:T(1024)} %param.6) | copy-start | bytes 24580
  32.6 40.5 %copy-start.4 = (f32[2048]{0:T(1024)S(1)}, f32[2048]{0:T(1024)}, u32[]{:S(2)}) copy-start(f32[2048]{0:T(1024)} %param.7) | copy-start | bytes 24580
  64.8 4.7 %copy-start = (f32[2048,512]{1,0:T(8,128)S(1)}, f32[2048,512]{1,0:T(8,128)}, u32[]{:S(2)}) copy-start(f32[2048,512]{1,0:T(8,128)} %gather_fusion) | copy-start | bytes 12582916
  64.8 8.3 %slice-start = ((s8[8388608]{0:T(1024)(128)(4,1)}), s8[4194304]{0:T(1024)(128)(4,1)S(1)}, s32[]{:S(2)}) async-start(s8[8388608]{0:T(1024)(128)(4,1)} %bitcast.324), calls=%async_computation.1 | async-start | bytes 8388608
  64.8 8.4 %copy-start.2 = (f32[2048,512]{1,0:T(8,128)S(1)}, f32[2048,512]{1,0:T(8,128)}, u32[]{:S(2)}) copy-start(f32[2048,512]{1,0:T(8,128)} %all-gather.10.cloned.1.call-done) | copy-start | bytes 12582916
  69.5 5.2 %slice-start.1 = ((s8[8388608]{0:T(1024)(128)(4,1)}), s8[4194304]{0:T(1024)(128)(4,1)S(1)}, s32[]{:S(2)}) async-start(s8[8388608]{0:T(1024)(128)(4,1)} %bitcast.324), calls=%async_computation.2 | async-start | bytes 8388608
Sparse Core Ops, SparseCore 0:
  10.4 54.3 all-gather.9
where the time goes:
time: 211 us
  matrix products  59.6 us (28%)
  blocking collectives  52.9 us (25%)
  other arithmetic  36.4 us (17%)
  waiting for transfers between devices  32.2 us (15%)
  local copies, waits for them, and re-layouts  15.8 us (7%)
  between operations  13.6 us (6%)
    dot_general x1, matrix products, block_stats(): lax.dot_general(units, rows, (((1,), (1,)), ((), ())), precision=lax.Prec...  59.6 us
    all_gather x4, blocking collectives, gathered_once(): both, at, found = (lax.all_gather(jnp.concatenate(lines), axis), 0, {})  52.9 us
    all_gather x1, waiting for transfers between devices, body(): lax.all_gather(units_mine, 'dp', axis=0, tiled=True)  32.2 us
    reduce_sum x1, other arithmetic, block_stats(): total = jnp.sum(jnp.exp(logits - peak[:, None]), axis=1)  15.2 us
    gather x1, local copies, waits for them, and re-layouts, body(): picked = jnp.take(normed, local_all, axis=0)  12.9 us
    mul x2, other arithmetic, unit_rows(): values * lax.rsqrt(jnp.sum(values * values, axis=-1, keepdims=True) + 1e-06)  5.9 us
    reduce_sum x2, other arithmetic, unit_rows(): jnp.sum(values * values, axis=-1, keepdims=True) + 1e-06  5.52 us
  transfers between devices with their start and end apart: 1, of which 1 were waited for; matrix products, arithmetic and copies ran while one was open for 10% of the time, Pallas kernels for 0%

commit v1 on v0

--- a/solution.py
+++ b/solution.py
@@ -1,3 +1,4 @@
+import functools
 import math
 import jax
 import jax.numpy as jnp
@@ -9,6 +10,16 @@
 MARGIN = 0.5
 COS_MARGIN = math.cos(MARGIN)
 SIN_MARGIN = math.sin(MARGIN)
+
+
+def pair_results(tile_in, dim_i):
+    world_n = lax.psum(1, axis_name="dp")
+    nodes = [world_n if w == dim_i else 1 for w in range(tile_in.ndim)]
+    ready = jnp.tile(tile_in, nodes)
+    return lax.all_to_all(ready, concat_axis=dim_i, tiled=True, split_axis=dim_i, axis_name="dp")
+
+
+read_threads = functools.partial(pair_results, dim_i=0)
 
 
 def gathered_once(shard, axis):
@@ -81,13 +92,7 @@
     count = labels.shape[0]
     picked = jnp.take(normed, local_all, axis=0)
     stats = block_stats(
-        lax.all_gather(units_mine, "dp", axis=0, tiled=True),
-        normed,
-        class_ids,
-        labels,
-        row_scale,
-        picked,
-        owned_all,
+        read_threads(units_mine), normed, class_ids, labels, row_scale, picked, owned_all
     )
     peak, total, target = tuple((fresh for fresh in stats))
     share = count // lax.axis_size(DP_CLS)

time: 211 us -> 202 us (0.957)
  between operations: 13.6 us -> 0.19 us
  waiting for transfers between devices: 32.2 us -> 24.1 us
  blocking collectives: 52.9 us -> 58.2 us
  starting transfers between devices: 0.01 us -> 4.85 us
    all_gather x1 -> x0, waiting for transfers between devices: 32.2 us -> none  [body(): lax.all_gather(units_mine, 'dp', axis=0, tiled=True)]
    all_to_all x0 -> x1, waiting for transfers between devices: none -> 24.1 us  [pair_results(): lax.all_to_all(ready, concat_axis=dim_i, tiled=True, split_axis=dim_i, ax...]
    all_gather x4, blocking collectives: 52.9 us -> 58.2 us  [gathered_once(): both, at, found = (lax.all_gather(jnp.concatenate(lines), axis), 0, {})]
    all_to_all x0 -> x1, starting transfers between devices: none -> 4.85 us  [pair_results(): lax.all_to_all(ready, concat_axis=dim_i, tiled=True, split_axis=dim_i, ax...]
    another operation x0 -> x1, local copies, waits for them, and re-layouts: none -> 2.51 us  [pair_results(): ready = jnp.tile(tile_in, nodes)]
  transfers between devices with their start and end apart: 1 -> 1, of which waited for: 1 -> 1; matrix products, arithmetic and copies ran while one was open for 10% -> 11% of each run, Pallas kernels for 0% -> 0%
where the time goes in v1:
time: 202 us
  matrix products  61.1 us (30%)
  blocking collectives  58.2 us (29%)
  other arithmetic  36.2 us (18%)
  waiting for transfers between devices  24.1 us (12%)
  local copies, waits for them, and re-layouts  16.8 us (8%)
  starting transfers between devices  4.85 us (2%)
    dot_general x1, matrix products, block_stats(): lax.dot_general(units, rows, (((1,), (1,)), ((), ())), precision=lax.Prec...  61.1 us
    all_gather x4, blocking collectives, gathered_once(): both, at, found = (lax.all_gather(jnp.concatenate(lines), axis), 0, {})  58.2 us
    all_to_all x1, waiting for transfers between devices, pair_results(): lax.all_to_all(ready, concat_axis=dim_i, tiled=True, split_axis=dim_i, ax...  24.1 us
    reduce_sum x1, other arithmetic, block_stats(): total = jnp.sum(jnp.exp(logits - peak[:, None]), axis=1)  15.2 us
    gather x1, local copies, waits for them, and re-layouts, body(): picked = jnp.take(normed, local_all, axis=0)  12.9 us
    mul x2, other arithmetic, unit_rows(): values * lax.rsqrt(jnp.sum(values * values, axis=-1, keepdims=True) + 1e-06)  7.15 us
    reduce_sum x2, other arithmetic, unit_rows(): jnp.sum(values * values, axis=-1, keepdims=True) + 1e-06  5.4 us
    all_to_all x1, starting transfers between devices, pair_results(): lax.all_to_all(ready, concat_axis=dim_i, tiled=True, split_axis=dim_i, ax...  4.85 us
  transfers between devices with their start and end apart: 1, of which 1 were waited for; matrix products, arithmetic and copies ran while one was open for 11% of the time, Pallas kernels for 0%

profile of v1, /device:TPU:1, one launch (start us, length us, event | category | flops | bytes accessed | tf_op | source)
XLA Modules:
  0.0 201.6 jit_solution(16188554033315869577)
XLA Ops:
  0.0 0.0 copy-start.1
  0.0 1.4 multiply_reduce_fusion.3
  1.4 1.4 broadcast_multiply_fusion.1
  2.8 2.5 %tile.2 = f32[4,512,512]{2,1,0:T(8,128)} broadcast(f32[512,512]{1,0:T(8,128)S(1)} %broadcast_multiply_fusion.1), dimensions={1,2} | broadcast | bytes 5242880 | tf_op jit(solution)/shard_map/tile | solution.py:18
  5.3 4.9 %all-to-all-start = ((f32[4,512,512]{2,1,0:T(8,128)}), f32[4,512,512]{2,1,0:T(8,128)}, u32[]{:S(2)}, u32[]{:S(2)}) async-start(f32[4,512,512]{2,1,0:T(8,128)} %tile.2), calls=%async_computation | async-start | bytes 8388608 | tf_op jit(solution)/shard_map/all_to_all | solution.py:19
  10.1 0.0 copy-done.1
  10.2 4.0 %multiply_reduce_fusion = f32[4096]{0:T(1024)S(1)} fusion(f32[4096,512]{1,0:T(8,128)} %param.5), kind=kLoop, calls=%fused_computation.4 | loop fusion | flops 4190208 | bytes 8404992 | tf_op jit(solution)/shard_map/reduce_sum | solution.py:52
  14.2 5.8 %broadcast_multiply_fusion = f32[4096,512]{1,0:T(8,128)} fusion(f32[4096,512]{1,0:T(8,128)} %param.5, f32[4096]{0:T(1024)S(1)} %add_rsqrt_fusion), kind=kLoop, calls=%fused_computation.7 | loop fusion | flops 2097152 | bytes 16793600 | tf_op jit(solution)/shard_map/mul | solution.py:52
  20.0 12.9 %gather_fusion = f32[2048,512]{1,0:T(8,128)} fusion(f32[4096,512]{1,0:T(8,128)} %broadcast_multiply_fusion, s32[2048]{0:T(1024)S(1)} %fusion.43), kind=kCustom, calls=%fused_computation | custom fusion | bytes 8396800 | tf_op jit(solution)/shard_map/jit(_take)/gather | solution.py:93
  32.9 24.1 %all-to-all-done = f32[4,512,512]{2,1,0:T(8,128)} async-done(((f32[4,512,512]{2,1,0:T(8,128)}), f32[4,512,512]{2,1,0:T(8,128)}, u32[]{:S(2)}, u32[]{:S(2)}) %all-to-all-start) | async-done | bytes 4194336 | tf_op jit(solution)/shard_map/all_to_all | solution.py:19
  57.1 0.0 copy-start
  57.1 0.0 copy-start.2
  57.1 0.0 slice-start
  57.1 4.0 %multiply_reduce_fusion.2 = f32[4,512]{1,0:T(4,128)S(1)} fusion(f32[4,512,512]{2,1,0:T(8,128)} %all-to-all-done, f32[4,512,512]{2,1,0:T(8,128)} %bitcast.331, pred[4,512]{1,0:T(4,128)(4,1)S(1)} %broadcast_in_dim.33), kind=kLoop, calls=%fused_computation.6 | loop fusion | flops 3143680 | bytes 8398848 | tf_op jit(solution)/shard_map/reduce_sum | solution.py:56
  61.1 0.6 copy-done
  61.7 0.0 slice-start.1
  61.7 3.1 %multiply_reduce_fusion.1 = f32[4,512]{1,0:T(4,128)S(1)} fusion(f32[4,512,512]{2,1,0:T(8,128)} %all-to-all-done, f32[4,512,512]{2,1,0:T(8,128)S(1)} %bitcast.332, f32[4,512]{1,0:T(4,128)S(1)} %multiply_reduce_fusion.2, pred[4,512]{1,0:T(4,128)(4,1)S(1)} %broadcast_in_dim.33), kind=kLoop, calls=%fused_computation.5 | loop fusion | flops 5240832 | bytes 8407040 | tf_op jit(solution)/shard_map/reduce_sum | solution.py:58
  64.9 0.0 copy-done.2
  64.9 0.0 slice-done
  64.9 0.8 slice-done.1
  65.7 61.1 %fusion = (f32[2048]{0:T(1024)S(1)}, f32[2048,4096]{1,0:T(8,128)}) fusion(f32[2048]{0:T(1024)S(1)} %copy-done.2, f32[2048]{0:T(1024)S(1)} %get-tuple-element.14, s32[4096]{0:T(1024)S(1)} %iota_add_fusion, s32[2048]{0:T(1024)S(1)} %copy-done.1, f32[2048,512]{1,0:T(8,128)} %bitcast.1, f32[4096,512]{1,0:T(8,128)S(1)} %bitcast.330), kind=kOutput, calls=%fused_computation.3 | convolution fusion | flops 51573161984 | bytes 46186496 | tf_op jit(solution)/shard_map/dot_general | solution.py:63
  126.8 15.2 %exponential_reduce_fusion = f32[2048]{0:T(1024)S(1)} fusion(f32[2048,4096]{1,0:T(8,128)} %get-tuple-element.21, f32[2048]{0:T(1024)S(1)} %get-tuple-element.20, f32[2048]{0:T(1024)S(1)} %copy-done.2, f32[2048]{0:T(1024)S(1)} %get-tuple-element.14, s32[4096]{0:T(1024)S(1)} %iota_add_fusion, s32[2048]{0:T(1024)S(1)} %copy-done.1), kind=kLoop, calls=%fused_computation.1 | loop fusion | flops 41940992 | bytes 33611776 | tf_op jit(solution)/shard_map/reduce_sum | solution.py:74
  142.0 9.1 %all-gather.4 = f32[4,3,2048]{2,1,0:T(4,128)S(1)} all-gather(f32[1,3,2048]{2,1,0:T(4,128)S(1)} %maximum_bitcast_fusion), channel_id=2, replica_groups=mesh['dp'=4,'cls_0'=8,'cls_1'=4,'cls_2'=2] {'dp'}, dimensions={0}, use_global_device_ids=true | all-gather | bytes 122880 | tf_op jit(solution)/shard_map/all_gather | solution.py:33
  151.2 0.1 fusion.35
  151.3 25.0 %all-gather.5 = f32[8,3,2048]{2,1,0:T(4,128)S(1)} all-gather(f32[1,3,2048]{2,1,0:T(4,128)S(1)} %maximum_bitcast_fusion.1), channel_id=3, replica_groups=mesh['dp'=4,'cls_0'=8,'cls_1'=4,'cls_2'=2] {'cls_0'}, dimensions={0}, use_global_device_ids=true | all-gather | bytes 221184 | tf_op jit(solution)/shard_map/all_gather | solution.py:33
  176.3 0.1 fusion.11
  176.4 0.2 fusion.13
  176.6 9.6 %all-gather.6 = f32[4,3,2048]{2,1,0:T(4,128)S(1)} all-gather(f32[1,3,2048]{2,1,0:T(4,128)S(1)} %maximum_bitcast_fusion.2), channel_id=4, replica_groups=mesh['dp'=4,'cls_0'=8,'cls_1'=4,'cls_2'=2] {'cls_1'}, dimensions={0}, use_global_device_ids=true | all-gather | bytes 122880 | tf_op jit(solution)/shard_map/all_gather | solution.py:33
  186.3 0.1 fusion.3
  186.4 14.5 %all-gather.7 = f32[2,3,2048]{2,1,0:T(4,128)S(1)} all-gather(f32[1,3,2048]{2,1,0:T(4,128)S(1)} %maximum_bitcast_fusion.3), channel_id=5, replica_groups=mesh['dp'=4,'cls_0'=8,'cls_1'=4,'cls_2'=2] {'cls_2'}, dimensions={0}, use_global_device_ids=true | all-gather | bytes 73728 | tf_op jit(solution)/shard_map/all_gather | solution.py:33
  201.0 0.6 dynamic-slice_subtract_fusion
  (19 shorter events, 0.3 us)
Async XLA Ops:
  0.0 10.1 %copy-start.1 = (s32[2048]{0:T(1024)S(1)}, s32[2048]{0:T(1024)}, u32[]{:S(2)}) copy-start(s32[2048]{0:T(1024)} %param.6) | copy-start | bytes 24580
  5.3 51.8 %all-to-all-start = ((f32[4,512,512]{2,1,0:T(8,128)}), f32[4,512,512]{2,1,0:T(8,128)}, u32[]{:S(2)}, u32[]{:S(2)}) async-start(f32[4,512,512]{2,1,0:T(8,128)} %tile.2), calls=%async_computation | async-start | bytes 8388608 | tf_op jit(solution)/shard_map/all_to_all | solution.py:19
  57.1 4.7 %copy-start = (f32[2048,512]{1,0:T(8,128)S(1)}, f32[2048,512]{1,0:T(8,128)}, u32[]{:S(2)}) copy-start(f32[2048,512]{1,0:T(8,128)} %gather_fusion) | copy-start | bytes 12582916
  57.1 7.8 %copy-start.2 = (f32[2048]{0:T(1024)S(1)}, f32[2048]{0:T(1024)}, u32[]{:S(2)}) copy-start(f32[2048]{0:T(1024)} %param.7) | copy-start | bytes 24580
  57.1 7.8 %slice-start = ((s8[8388608]{0:T(1024)(128)(4,1)}), s8[4194304]{0:T(1024)(128)(4,1)S(1)}, s32[]{:S(2)}) async-start(s8[8388608]{0:T(1024)(128)(4,1)} %bitcast.329), calls=%async_computation.1 | async-start | bytes 8388608
  61.7 4.0 %slice-start.1 = ((s8[8388608]{0:T(1024)(128)(4,1)}), s8[4194304]{0:T(1024)(128)(4,1)S(1)}, s32[]{:S(2)}) async-start(s8[8388608]{0:T(1024)(128)(4,1)} %bitcast.329), calls=%async_computation.2 | async-start | bytes 8388608
